TPU v7x, 32 devices: a whole 2x2x4 slice. The times are simulated.
32 devices in a mesh: gx: 8 (over z, x), gy: 4 (over y, core).
Axes of the slice: x: 2, y: 2, z: 4, core: 2. Of those that a mesh axis runs over, the one named last changes fastest.
Arguments:
- activations: bfloat16 [64, 65536], P('gx', 'gy'), may hold values from -6 to 6
- live_blocks: int32 [4, 8, 512], P(None, 'gx', 'gy'), may hold values 0 or 1
- tile_index: int32 [4, 512, 8], replicated, may hold values from 0 to 511, as said below
- tile_count: int32 [4, 4, 128], P(None, 'gy', 'gx'), may hold values from 1 to 8, as said below
- weight_tiles: bfloat16 [4, 4, 128, 8, 128, 128], P(None, 'gy', 'gx'), may hold values from -0.375 to 0.375
- bias_terms: float32 [4, 4, 128, 128], P(None, 'gy', 'gx'), may hold values from -2 to 2
Outputs:
- final_layer: bfloat16 [64, 65536], P('gx', 'gy')
Inputs may be any that keep to these rules, and one draw needn't show every extreme that they name: The input block of slot t lies in group t mod 4: tile_index[l, j, t] divided by 128, rounded down, equals t mod 4. Of the 16 blocks g * 128 + r * 16 + k (k < 16) held by the device with index r of gx and g of gy, at most one has tile_count above 4 in each layer; in every layer some device has such a block with exactly 8 used slots.
All inputs are finite; a program needn't handle non-finite values. No bound on the sum of `live_blocks` on one device may be relied on, other than what follows from the above.
Results may differ from a plain program's by a relative error of at most 0.0057.
Values may be sent and summed in bfloat16 or wider, within the bound.
No kernel may reach another device: no remote copies, remote signals or barrier semaphores. Data moves between devices by JAX's collectives and lax.ppermute only.
A program may use at most 64 MiB of HBM per device.

v0:
```python
import jax
import jax.numpy as jnp
from jax import lax
from jax.sharding import PartitionSpec as P

LAYERS = 4


def local(activations, live_blocks, tile_index, tile_count, weight_tiles, bias_terms):
    across = lax.axis_size("gx")
    groups = lax.axis_size("gy")
    my_group = lax.axis_index("gy")
    row_count = activations.shape[0]
    tile_side = weight_tiles.shape[-1]
    group_blocks = activations.shape[1] // tile_side
    owned_blocks = weight_tiles.shape[2]
    tile_depth = weight_tiles.shape[3]
    slab_count = tile_depth // groups
    device_count = across * groups
    count_table = lax.all_gather(tile_count, ("gx", "gy"), axis=1, tiled=True)
    current = activations
    for layer_index in range(LAYERS):
        kept_mask = live_blocks[layer_index, 0].astype(jnp.bfloat16)
        blocks = current.reshape(row_count, group_blocks, tile_side) * kept_mask[None, :, None]
        tile_table = tile_index[layer_index].reshape(
            groups, across, owned_blocks, slab_count, groups
        )
        picked = lax.dynamic_index_in_dim(tile_table, my_group, 4, keepdims=False)
        picked_all = jnp.transpose(picked, (1, 0, 2, 3)) - my_group * group_blocks
        chosen = picked_all[:, :, :, 0]
        outgoing = jnp.take(blocks, chosen.reshape(-1), axis=1)
        outgoing = outgoing.reshape(row_count, device_count, owned_blocks, tile_side)
        incoming = lax.all_to_all(outgoing, ("gx", "gy"), split_axis=1, concat_axis=1, tiled=True)
        incoming = incoming.reshape(row_count, across, groups, owned_blocks, tile_side)
        counts = tile_count[layer_index, 0]
        usable = (jnp.arange(tile_depth, dtype=jnp.int32)[None, :] < counts[:, None]).astype(
            jnp.bfloat16
        )
        weights = weight_tiles[layer_index, 0] * usable[:, :, None, None]
        weights = weights.reshape(owned_blocks, slab_count, groups, tile_side, tile_side)
        summed = jnp.einsum(
            "rapki,kpij->rakj", incoming, weights[:, 0], preferred_element_type=jnp.float32
        )
        heavy_all = jnp.argmax(count_table[layer_index], axis=1)
        rest_ids = jnp.take_along_axis(
            picked_all.reshape(device_count, owned_blocks, slab_count),
            heavy_all[:, None, None],
            axis=1,
        )[:, 0, 1:]
        rest_out = jnp.take(blocks, rest_ids.reshape(-1), axis=1).reshape(
            row_count, device_count, slab_count - 1, tile_side
        )
        rest_in = lax.all_to_all(rest_out, ("gx", "gy"), split_axis=1, concat_axis=1, tiled=True)
        rest_in = rest_in.reshape(row_count, across, groups, slab_count - 1, tile_side)
        heavy_here = jnp.argmax(counts)
        rest_weights = lax.dynamic_index_in_dim(weights, heavy_here, 0, keepdims=False)[1:]
        extra = jnp.einsum(
            "rapsi,spij->raj", rest_in, rest_weights, preferred_element_type=jnp.float32
        )
        selector = (jnp.arange(owned_blocks, dtype=jnp.int32) == heavy_here).astype(jnp.float32)
        summed = summed + selector[None, None, :, None] * extra[:, :, None, :]
        shifted = summed + bias_terms[layer_index, 0][None, None]
        result = (
            jax.nn.relu(shifted)
            .astype(jnp.bfloat16)
            .reshape(row_count, across, owned_blocks * tile_side)
        )
        returned = lax.all_to_all(result, "gx", split_axis=1, concat_axis=1, tiled=True)
        current = returned.reshape(row_count, group_blocks * tile_side)
    return current


def solution(mesh):
    placed = (
        P("gx", "gy"),
        P(None, "gx", "gy"),
        P(),
        P(None, "gy", "gx"),
        P(None, "gy", "gx", None, None, None),
        P(None, "gy", "gx", None),
    )
    return jax.shard_map(
        local, mesh=mesh, in_specs=placed, out_specs=P("gx", "gy"), check_vma=False
    )
```

profile of v0, /device:TPU:0, one launch (start us, length us, event | category | flops | bytes accessed | tf_op | source)
XLA Modules:
  0.0 289.5 jit_solution(15461610320700656826)
XLA Ops:
  0.0 43.6 %all_gather.3 = s32[4,32,16]{2,0,1:T(4,128)S(1)} all-gather(s32[4,1,16]{2,0,1:T(4,128)} %bitcast.395), channel_id=1, replica_groups=mesh['gx'=8,'gy'=4] {'gx','gy'}, dimensions={1}, use_global_device_ids=true | all-gather | bytes 8448 | tf_op jit(solution)/shard_map/all_gather | solution.py:20
  45.7 0.8 fusion.42
  48.1 0.7 gather_fusion.1
  49.0 1.1 bitcast_multiply_fusion
  50.7 0.7 select_bitcast_fusion.3
  51.4 2.6 all-to-all-start.1
  54.0 0.7 slice_bitcast_fusion.56
  54.7 1.4 iota_reduce_fusion.7
  56.2 1.8 gather_fusion
  58.3 1.8 broadcast_select_fusion.3
  60.1 1.2 copy.89
  61.4 5.7 %all-to-all-start = ((bf16[8,32,16,128]{3,2,0,1:T(8,128)(2,1)}), bf16[8,32,16,128]{3,2,0,1:T(8,128)(2,1)S(1)}, u32[]{:S(2)}, u32[]{:S(2)}) async-start(bf16[8,32,16,128]{3,2,0,1:T(8,128)(2,1)} %copy.89), calls=%async_computation | async-start | bytes 2097152 | tf_op jit(solution)/shard_map/all_to_all | solution.py:33
  69.5 0.7 gather_fusion.4
  71.1 11.1 %fusion.40 = (bf16[1,1,16,8,128,128]{5,4,3,2,1,0:T(8,128)(2,1)S(1)}, bf16[1,1,16,8,128,128]{5,4,3,2,1,0:T(8,128)(2,1)}, bf16[1,1,16,8,128,128]{5,4,3,2,1,0:T(8,128)(2,1)}, bf16[1,1,16,8,128,128]{5,4,3,2,1,0:T(8,128)(2,1)}) fusion(bf16[4,1,16,8,128,128]{5,4,3,2,1,0:T(8,128)(2,1)} %param.16), kind=kLoop, calls=%fused_computation.161 | loop fusion | bytes 33554432 | tf_op jit(solution)/shard_map/slice | solution.py:39
  82.5 1.9 copy-done.1
  84.7 8.7 %all-to-all-done = bf16[8,32,16,128]{3,2,0,1:T(8,128)(2,1)S(1)} async-done(((bf16[8,32,16,128]{3,2,0,1:T(8,128)(2,1)}), bf16[8,32,16,128]{3,2,0,1:T(8,128)(2,1)S(1)}, u32[]{:S(2)}, u32[]{:S(2)}) %all-to-all-start) | async-done | bytes 1048608 | tf_op jit(solution)/shard_map/all_to_all | solution.py:33
  93.3 3.0 %fusion.23 = bf16[8,8,16,128]{3,1,0,2:T(8,128)(2,1)S(1)} fusion(bf16[16,2,4,128,128]{4,3,2,0,1:T(8,128)(2,1)} %copy-done.1, bf16[8,8,4,16,128]{4,3,0,2,1:T(8,128)(2,1)S(1)} %bitcast.371, f32[16,128]{1,0:T(8,128)S(1)} %get-tuple-element.46, f32[8,8,128]{2,1,0:T(8,128)S(1)} %convolution_bitcast_fusion.3, f32[16]{0:T(128)S(1)} %compare_convert_fusion.7), kind=kOutput, calls=%fused_computation.43 | convolution fusion | flops 134873088 | bytes 3448896 | tf_op jit(solution)/shard_map/rapki,kpij->rakj/dot_general | solution.py:41
  96.5 0.8 reshape.513
  97.3 3.6 %all-to-all-start.2 = ((bf16[8,8,2048]{2,0,1:T(8,128)(2,1)}), bf16[8,8,2048]{2,0,1:T(8,128)(2,1)S(1)}, u32[]{:S(2)}, u32[]{:S(2)}) async-start(bf16[8,8,2048]{2,0,1:T(8,128)(2,1)} %reshape.513), calls=%async_computation.2 | async-start | bytes 524288 | tf_op jit(solution)/shard_map/all_to_all | solution.py:68
  101.0 9.1 %all-to-all-done.2 = bf16[8,8,2048]{2,0,1:T(8,128)(2,1)S(1)} async-done(((bf16[8,8,2048]{2,0,1:T(8,128)(2,1)}), bf16[8,8,2048]{2,0,1:T(8,128)(2,1)S(1)}, u32[]{:S(2)}, u32[]{:S(2)}) %all-to-all-start.2) | async-done | bytes 262176 | tf_op jit(solution)/shard_map/all_to_all | solution.py:68
  110.3 1.8 gather_fusion.3
  112.7 0.7 select_bitcast_fusion.2
  113.5 3.6 %all-to-all-start.4 = ((bf16[8,32,1,128]{3,0,2,1:T(8,128)(2,1)}), bf16[8,32,1,128]{3,0,2,1:T(8,128)(2,1)S(1)}, u32[]{:S(2)}, u32[]{:S(2)}) async-start(bf16[8,32,1,128]{3,0,2,1:T(8,128)(2,1)} %select_bitcast_fusion.2), calls=%async_computation.4 | async-start | bytes 131072 | tf_op jit(solution)/shard_map/all_to_all | solution.py:53
  117.1 1.8 broadcast_select_fusion.2
  118.8 1.3 copy.101
  120.1 4.4 %all-to-all-done.4 = bf16[8,32,1,128]{3,0,2,1:T(8,128)(2,1)S(1)} async-done(((bf16[8,32,1,128]{3,0,2,1:T(8,128)(2,1)}), bf16[8,32,1,128]{3,0,2,1:T(8,128)(2,1)S(1)}, u32[]{:S(2)}, u32[]{:S(2)}) %all-to-all-start.4) | async-done | bytes 65568 | tf_op jit(solution)/shard_map/all_to_all | solution.py:53
  124.5 2.8 all-to-all-start.3
  129.7 0.7 gather_fusion.7
  131.7 2.5 copy_multiply_fusion.1
  134.3 2.0 copy-done.2
  136.4 16.9 %all-to-all-done.3 = bf16[8,32,16,128]{3,2,0,1:T(8,128)(2,1)S(1)} async-done(((bf16[8,32,16,128]{3,2,0,1:T(8,128)(2,1)}), bf16[8,32,16,128]{3,2,0,1:T(8,128)(2,1)S(1)}, u32[]{:S(2)}, u32[]{:S(2)}) %all-to-all-start.3) | async-done | bytes 1048608 | tf_op jit(solution)/shard_map/all_to_all | solution.py:33
  153.3 3.0 %fusion.22 = bf16[8,8,16,128]{3,1,0,2:T(8,128)(2,1)S(1)} fusion(bf16[16,2,4,128,128]{4,3,2,0,1:T(8,128)(2,1)} %copy-done.2, bf16[8,8,4,16,128]{4,3,0,2,1:T(8,128)(2,1)S(1)} %bitcast.370, f32[16,128]{1,0:T(8,128)S(1)} %get-tuple-element.45, f32[8,8,128]{2,1,0:T(8,128)S(1)} %convolution_bitcast_fusion.2, f32[16]{0:T(128)S(1)} %compare_convert_fusion.6), kind=kOutput, calls=%fused_computation.42 | convolution fusion | flops 134873088 | bytes 3448896 | tf_op jit(solution)/shard_map/rapki,kpij->rakj/dot_general | solution.py:41
  156.5 0.8 reshape.514
  157.3 3.5 %all-to-all-start.5 = ((bf16[8,8,2048]{2,0,1:T(8,128)(2,1)}), bf16[8,8,2048]{2,0,1:T(8,128)(2,1)S(1)}, u32[]{:S(2)}, u32[]{:S(2)}) async-start(bf16[8,8,2048]{2,0,1:T(8,128)(2,1)} %reshape.514), calls=%async_computation.5 | async-start | bytes 524288 | tf_op jit(solution)/shard_map/all_to_all | solution.py:68
  161.0 9.0 %all-to-all-done.5 = bf16[8,8,2048]{2,0,1:T(8,128)(2,1)S(1)} async-done(((bf16[8,8,2048]{2,0,1:T(8,128)(2,1)}), bf16[8,8,2048]{2,0,1:T(8,128)(2,1)S(1)}, u32[]{:S(2)}, u32[]{:S(2)}) %all-to-all-start.5) | async-done | bytes 262176 | tf_op jit(solution)/shard_map/all_to_all | solution.py:68
  170.2 1.8 gather_fusion.6
  172.6 0.7 select_bitcast_fusion.1
  173.3 3.6 %all-to-all-start.7 = ((bf16[8,32,1,128]{3,0,2,1:T(8,128)(2,1)}), bf16[8,32,1,128]{3,0,2,1:T(8,128)(2,1)S(1)}, u32[]{:S(2)}, u32[]{:S(2)}) async-start(bf16[8,32,1,128]{3,0,2,1:T(8,128)(2,1)} %select_bitcast_fusion.1), calls=%async_computation.7 | async-start | bytes 131072 | tf_op jit(solution)/shard_map/all_to_all | solution.py:53
  176.9 1.8 broadcast_select_fusion.1
  178.7 1.3 copy.112
  180.0 4.3 %all-to-all-done.7 = bf16[8,32,1,128]{3,0,2,1:T(8,128)(2,1)S(1)} async-done(((bf16[8,32,1,128]{3,0,2,1:T(8,128)(2,1)}), bf16[8,32,1,128]{3,0,2,1:T(8,128)(2,1)S(1)}, u32[]{:S(2)}, u32[]{:S(2)}) %all-to-all-start.7) | async-done | bytes 65568 | tf_op jit(solution)/shard_map/all_to_all | solution.py:53
  184.3 2.6 all-to-all-start.6
  187.0 0.7 iota_reduce_fusion.5
  189.2 0.7 gather_fusion.10
  191.3 2.5 copy_multiply_fusion.2
  193.8 2.0 copy-done.3
  196.0 17.2 %all-to-all-done.6 = bf16[8,32,16,128]{3,2,0,1:T(8,128)(2,1)S(1)} async-done(((bf16[8,32,16,128]{3,2,0,1:T(8,128)(2,1)}), bf16[8,32,16,128]{3,2,0,1:T(8,128)(2,1)S(1)}, u32[]{:S(2)}, u32[]{:S(2)}) %all-to-all-start.6) | async-done | bytes 1048608 | tf_op jit(solution)/shard_map/all_to_all | solution.py:33
  213.2 3.0 %fusion.21 = bf16[8,8,16,128]{3,1,0,2:T(8,128)(2,1)S(1)} fusion(bf16[16,2,4,128,128]{4,3,2,0,1:T(8,128)(2,1)} %copy-done.3, bf16[8,8,4,16,128]{4,3,0,2,1:T(8,128)(2,1)S(1)} %bitcast.372, f32[16,128]{1,0:T(8,128)S(1)} %get-tuple-element.47, f32[8,8,128]{2,1,0:T(8,128)S(1)} %convolution_bitcast_fusion.1, f32[16]{0:T(128)S(1)} %compare_convert_fusion.5), kind=kOutput, calls=%fused_computation.41 | convolution fusion | flops 134873088 | bytes 3448896 | tf_op jit(solution)/shard_map/rapki,kpij->rakj/dot_general | solution.py:41
  216.4 0.8 reshape.515
  217.2 3.5 %all-to-all-start.8 = ((bf16[8,8,2048]{2,0,1:T(8,128)(2,1)}), bf16[8,8,2048]{2,0,1:T(8,128)(2,1)S(1)}, u32[]{:S(2)}, u32[]{:S(2)}) async-start(bf16[8,8,2048]{2,0,1:T(8,128)(2,1)} %reshape.515), calls=%async_computation.8 | async-start | bytes 524288 | tf_op jit(solution)/shard_map/all_to_all | solution.py:68
  220.7 9.1 %all-to-all-done.8 = bf16[8,8,2048]{2,0,1:T(8,128)(2,1)S(1)} async-done(((bf16[8,8,2048]{2,0,1:T(8,128)(2,1)}), bf16[8,8,2048]{2,0,1:T(8,128)(2,1)S(1)}, u32[]{:S(2)}, u32[]{:S(2)}) %all-to-all-start.8) | async-done | bytes 262176 | tf_op jit(solution)/shard_map/all_to_all | solution.py:68
  230.0 1.8 gather_fusion.9
  232.4 0.7 select_bitcast_fusion
  233.2 3.6 %all-to-all-start.10 = ((bf16[8,32,1,128]{3,0,2,1:T(8,128)(2,1)}), bf16[8,32,1,128]{3,0,2,1:T(8,128)(2,1)S(1)}, u32[]{:S(2)}, u32[]{:S(2)}) async-start(bf16[8,32,1,128]{3,0,2,1:T(8,128)(2,1)} %select_bitcast_fusion), calls=%async_computation.10 | async-start | bytes 131072 | tf_op jit(solution)/shard_map/all_to_all | solution.py:53
  236.8 1.8 broadcast_select_fusion
  238.6 1.2 copy.123
  239.8 4.4 %all-to-all-done.10 = bf16[8,32,1,128]{3,0,2,1:T(8,128)(2,1)S(1)} async-done(((bf16[8,32,1,128]{3,0,2,1:T(8,128)(2,1)}), bf16[8,32,1,128]{3,0,2,1:T(8,128)(2,1)S(1)}, u32[]{:S(2)}, u32[]{:S(2)}) %all-to-all-start.10) | async-done | bytes 65568 | tf_op jit(solution)/shard_map/all_to_all | solution.py:53
  244.2 2.6 all-to-all-start.9
  250.1 2.5 copy_multiply_fusion.3
  252.6 1.9 copy-done
  254.7 18.3 %all-to-all-done.9 = bf16[8,32,16,128]{3,2,0,1:T(8,128)(2,1)S(1)} async-done(((bf16[8,32,16,128]{3,2,0,1:T(8,128)(2,1)}), bf16[8,32,16,128]{3,2,0,1:T(8,128)(2,1)S(1)}, u32[]{:S(2)}, u32[]{:S(2)}) %all-to-all-start.9) | async-done | bytes 1048608 | tf_op jit(solution)/shard_map/all_to_all | solution.py:33
  273.1 3.0 %fusion.20 = bf16[8,8,16,128]{3,1,0,2:T(8,128)(2,1)S(1)} fusion(bf16[16,2,4,128,128]{4,3,2,0,1:T(8,128)(2,1)} %copy-done, bf16[8,8,4,16,128]{4,3,0,2,1:T(8,128)(2,1)S(1)} %bitcast.373, f32[16,128]{1,0:T(8,128)S(1)} %get-tuple-element.44, f32[8,8,128]{2,1,0:T(8,128)S(1)} %convolution_bitcast_fusion, f32[16]{0:T(128)S(1)} %compare_convert_fusion.4), kind=kOutput, calls=%fused_computation.40 | convolution fusion | flops 134873088 | bytes 3448896 | tf_op jit(solution)/shard_map/rapki,kpij->rakj/dot_general | solution.py:41
  276.3 12.5 %all_to_all.60 = bf16[8,8,2048]{2,0,1:T(8,128)(2,1)S(1)} all-to-all(bf16[8,8,2048]{2,0,1:T(8,128)(2,1)S(1)} %reshape.516), channel_id=1, replica_groups=mesh['gx'=8,'gy'=4] {'gx'}, dimensions={1} | all-to-all | bytes 524288 | tf_op jit(solution)/shard_map/all_to_all | solution.py:68
  288.8 0.7 copy.197
  (102 shorter events, 14.5 us)
Async XLA Ops:
  51.4 10.0 %all-to-all-start.1 = ((bf16[8,32,1,128]{3,0,2,1:T(8,128)(2,1)}), bf16[8,32,1,128]{3,0,2,1:T(8,128)(2,1)S(1)}, u32[]{:S(2)}, u32[]{:S(2)}) async-start(bf16[8,32,1,128]{3,0,2,1:T(8,128)(2,1)} %select_bitcast_fusion.3), calls=%async_computation.1 | async-start | bytes 131072 | tf_op jit(solution)/shard_map/all_to_all | solution.py:53
  56.2 14.9 %copy-start.4 = (f32[4,1,16,128]{3,2,1,0:T(8,128)S(1)}, f32[4,1,16,128]{3,2,1,0:T(8,128)}, u32[]{:S(2)}) copy-start(f32[4,1,16,128]{3,2,1,0:T(8,128)} %param.17) | copy-start | bytes 98308
  61.4 31.9 %all-to-all-start = ((bf16[8,32,16,128]{3,2,0,1:T(8,128)(2,1)}), bf16[8,32,16,128]{3,2,0,1:T(8,128)(2,1)S(1)}, u32[]{:S(2)}, u32[]{:S(2)}) async-start(bf16[8,32,16,128]{3,2,0,1:T(8,128)(2,1)} %copy.89), calls=%async_computation | async-start | bytes 2097152 | tf_op jit(solution)/shard_map/all_to_all | solution.py:33
  82.5 2.0 copy-start.1
  97.3 12.8 %all-to-all-start.2 = ((bf16[8,8,2048]{2,0,1:T(8,128)(2,1)}), bf16[8,8,2048]{2,0,1:T(8,128)(2,1)S(1)}, u32[]{:S(2)}, u32[]{:S(2)}) async-start(bf16[8,8,2048]{2,0,1:T(8,128)(2,1)} %reshape.513), calls=%async_computation.2 | async-start | bytes 524288 | tf_op jit(solution)/shard_map/all_to_all | solution.py:68
  110.3 17.0 %copy-start.5 = (s32[4,1,16]{2,1,0:T(1,128)S(1)}, s32[4,1,16]{2,1,0:T(1,128)}, u32[]{:S(2)}) copy-start(s32[4,1,16]{2,1,0:T(1,128)} %param.15) | copy-start | bytes 772
  113.5 11.0 %all-to-all-start.4 = ((bf16[8,32,1,128]{3,0,2,1:T(8,128)(2,1)}), bf16[8,32,1,128]{3,0,2,1:T(8,128)(2,1)S(1)}, u32[]{:S(2)}, u32[]{:S(2)}) async-start(bf16[8,32,1,128]{3,0,2,1:T(8,128)(2,1)} %select_bitcast_fusion.2), calls=%async_computation.4 | async-start | bytes 131072 | tf_op jit(solution)/shard_map/all_to_all | solution.py:53
  124.5 28.8 %all-to-all-start.3 = ((bf16[8,32,16,128]{3,2,0,1:T(8,128)(2,1)}), bf16[8,32,16,128]{3,2,0,1:T(8,128)(2,1)S(1)}, u32[]{:S(2)}, u32[]{:S(2)}) async-start(bf16[8,32,16,128]{3,2,0,1:T(8,128)(2,1)} %copy.101), calls=%async_computation.3 | async-start | bytes 2097152 | tf_op jit(solution)/shard_map/all_to_all | solution.py:33
  134.3 2.0 copy-start.2
  157.3 12.7 %all-to-all-start.5 = ((bf16[8,8,2048]{2,0,1:T(8,128)(2,1)}), bf16[8,8,2048]{2,0,1:T(8,128)(2,1)S(1)}, u32[]{:S(2)}, u32[]{:S(2)}) async-start(bf16[8,8,2048]{2,0,1:T(8,128)(2,1)} %reshape.514), calls=%async_computation.5 | async-start | bytes 524288 | tf_op jit(solution)/shard_map/all_to_all | solution.py:68
  173.3 11.0 %all-to-all-start.7 = ((bf16[8,32,1,128]{3,0,2,1:T(8,128)(2,1)}), bf16[8,32,1,128]{3,0,2,1:T(8,128)(2,1)S(1)}, u32[]{:S(2)}, u32[]{:S(2)}) async-start(bf16[8,32,1,128]{3,0,2,1:T(8,128)(2,1)} %select_bitcast_fusion.1), calls=%async_computation.7 | async-start | bytes 131072 | tf_op jit(solution)/shard_map/all_to_all | solution.py:53
  184.3 28.8 %all-to-all-start.6 = ((bf16[8,32,16,128]{3,2,0,1:T(8,128)(2,1)}), bf16[8,32,16,128]{3,2,0,1:T(8,128)(2,1)S(1)}, u32[]{:S(2)}, u32[]{:S(2)}) async-start(bf16[8,32,16,128]{3,2,0,1:T(8,128)(2,1)} %copy.112), calls=%async_computation.6 | async-start | bytes 2097152 | tf_op jit(solution)/shard_map/all_to_all | solution.py:33
  193.8 2.0 copy-start.3
  217.2 12.7 %all-to-all-start.8 = ((bf16[8,8,2048]{2,0,1:T(8,128)(2,1)}), bf16[8,8,2048]{2,0,1:T(8,128)(2,1)S(1)}, u32[]{:S(2)}, u32[]{:S(2)}) async-start(bf16[8,8,2048]{2,0,1:T(8,128)(2,1)} %reshape.515), calls=%async_computation.8 | async-start | bytes 524288 | tf_op jit(solution)/shard_map/all_to_all | solution.py:68
  233.2 11.0 %all-to-all-start.10 = ((bf16[8,32,1,128]{3,0,2,1:T(8,128)(2,1)}), bf16[8,32,1,128]{3,0,2,1:T(8,128)(2,1)S(1)}, u32[]{:S(2)}, u32[]{:S(2)}) async-start(bf16[8,32,1,128]{3,0,2,1:T(8,128)(2,1)} %select_bitcast_fusion), calls=%async_computation.10 | async-start | bytes 131072 | tf_op jit(solution)/shard_map/all_to_all | solution.py:53
  244.2 28.8 %all-to-all-start.9 = ((bf16[8,32,16,128]{3,2,0,1:T(8,128)(2,1)}), bf16[8,32,16,128]{3,2,0,1:T(8,128)(2,1)S(1)}, u32[]{:S(2)}, u32[]{:S(2)}) async-start(bf16[8,32,16,128]{3,2,0,1:T(8,128)(2,1)} %copy.123), calls=%async_computation.9 | async-start | bytes 2097152 | tf_op jit(solution)/shard_map/all_to_all | solution.py:33
  252.6 1.9 copy-start
where the time goes:
time: 291 us; the launch traced here: 289 us
  waiting for transfers between devices  102 us (35%)
  blocking collectives  56.1 us (19%)
  local copies, waits for them, and re-layouts  44 us (15%)
  starting transfers between devices  37.9 us (13%)
  other arithmetic  29.1 us (10%)
  matrix products  12.6 us (4%)
  between operations  8.25 us (3%)
    all_to_all x4, waiting for transfers between devices, local(): lax.all_to_all(outgoing, ('gx', 'gy'), split_axis=1, concat_axis=1, tiled...  61.2 us
    all_gather x1, blocking collectives, local(): count_table = lax.all_gather(tile_count, ('gx', 'gy'), axis=1, tiled=True)  43.6 us
    all_to_all x3, waiting for transfers between devices, local(): lax.all_to_all(result, 'gx', split_axis=1, concat_axis=1, tiled=True)  27.2 us
    all_to_all x4, starting transfers between devices, local(): lax.all_to_all(outgoing, ('gx', 'gy'), split_axis=1, concat_axis=1, tiled...  13.8 us
    all_to_all x4, starting transfers between devices, local(): lax.all_to_all(rest_out, ('gx', 'gy'), split_axis=1, concat_axis=1, tiled...  13.4 us
    all_to_all x4, waiting for transfers between devices, local(): lax.all_to_all(rest_out, ('gx', 'gy'), split_axis=1, concat_axis=1, tiled...  13.3 us
    all_to_all x1, blocking collectives, local(): lax.all_to_all(result, 'gx', split_axis=1, concat_axis=1, tiled=True)  12.5 us
    dot_general x4, matrix products, local(): jnp.einsum('rapki,kpij->rakj', incoming, weights[:, 0], preferred_element...  12 us
  transfers between devices with their start and end apart: 11, of which 11 were waited for; matrix products, arithmetic and copies ran while one was open for 15% of the time, Pallas kernels for 0%

commit v1 on v0

--- a/solution.py
+++ b/solution.py
@@ -65,7 +65,9 @@
             .astype(jnp.bfloat16)
             .reshape(row_count, across, owned_blocks * tile_side)
         )
-        returned = lax.all_to_all(result, "gx", split_axis=1, concat_axis=1, tiled=True)
+        shards = jnp.split(result, lax.axis_size("gx"), axis=1)
+        received = lax.all_to_all(jnp.stack(shards), "gx", 0, 0)
+        returned = jnp.concatenate(received, axis=1)
         current = returned.reshape(row_count, group_blocks * tile_side)
     return current
 

time: 291 us -> 305 us (1.048)
  local copies, waits for them, and re-layouts: 44 us -> 58.3 us
    unnamed x17 -> x45, local copies, waits for them, and re-layouts: 8.55 us -> 22.1 us
    reshape x8 -> x4, local copies, waits for them, and re-layouts: 3.26 us -> 0.18 us  [local(): result = jax.nn.relu(shifted).astype(jnp.bfloat16).reshape(row_count, acr...]
where the time goes in v1:
time: 305 us; the launch traced here: 304 us
  waiting for transfers between devices  101 us (33%)
  local copies, waits for them, and re-layouts  58.3 us (19%)
  blocking collectives  56.1 us (18%)
  starting transfers between devices  38.1 us (12%)
  other arithmetic  29.1 us (10%)
  matrix products  12.6 us (4%)
  between operations  8.34 us (3%)
    all_to_all x4, waiting for transfers between devices, local(): lax.all_to_all(outgoing, ('gx', 'gy'), split_axis=1, concat_axis=1, tiled...  60.9 us
    all_gather x1, blocking collectives, local(): count_table = lax.all_gather(tile_count, ('gx', 'gy'), axis=1, tiled=True)  43.6 us
    all_to_all x3, waiting for transfers between devices, local(): received = lax.all_to_all(jnp.stack(shards), 'gx', 0, 0)  27.2 us
    unnamed x45, local copies, waits for them, and re-layouts  22.1 us
    all_to_all x4, starting transfers between devices, local(): lax.all_to_all(outgoing, ('gx', 'gy'), split_axis=1, concat_axis=1, tiled...  14 us
    all_to_all x4, starting transfers between devices, local(): lax.all_to_all(rest_out, ('gx', 'gy'), split_axis=1, concat_axis=1, tiled...  13.4 us
    all_to_all x4, waiting for transfers between devices, local(): lax.all_to_all(rest_out, ('gx', 'gy'), split_axis=1, concat_axis=1, tiled...  13.3 us
    all_to_all x1, blocking collectives, local(): received = lax.all_to_all(jnp.stack(shards), 'gx', 0, 0)  12.5 us
  transfers between devices with their start and end apart: 11, of which 11 were waited for; matrix products, arithmetic and copies ran while one was open for 15% of the time, Pallas kernels for 0%

profile of v1, /device:TPU:0, one launch (start us, length us, event | category | flops | bytes accessed | tf_op | source)
XLA Modules:
  0.0 303.9 jit_solution(16517142687306011255)
XLA Ops:
  0.0 43.6 %all_gather.3 = s32[4,32,16]{2,0,1:T(4,128)S(1)} all-gather(s32[4,1,16]{2,0,1:T(4,128)} %bitcast.491), channel_id=1, replica_groups=mesh['gx'=8,'gy'=4] {'gx','gy'}, dimensions={1}, use_global_device_ids=true | all-gather | bytes 8448 | tf_op jit(solution)/shard_map/all_gather | solution.py:20
  45.0 0.7 convert.6
  45.7 0.8 fusion.50
  48.1 0.7 gather_fusion.1
  49.0 1.1 bitcast_multiply_fusion
  50.7 0.7 select_bitcast_fusion.3
  51.4 2.6 all-to-all-start.1
  54.0 0.7 slice_bitcast_fusion.64
  54.7 1.4 iota_reduce_fusion.7
  56.2 1.8 gather_fusion
  58.3 1.8 broadcast_select_fusion.3
  60.1 1.2 copy.483
  61.4 5.7 %all-to-all-start = ((bf16[8,32,16,128]{3,2,0,1:T(8,128)(2,1)}), bf16[8,32,16,128]{3,2,0,1:T(8,128)(2,1)S(1)}, u32[]{:S(2)}, u32[]{:S(2)}) async-start(bf16[8,32,16,128]{3,2,0,1:T(8,128)(2,1)} %copy.483), calls=%async_computation | async-start | bytes 2097152 | tf_op jit(solution)/shard_map/all_to_all | solution.py:33
  67.1 0.7 compare_convert_fusion.7
  69.5 0.7 gather_fusion.4
  71.1 11.1 %fusion.44 = (bf16[1,1,16,8,128,128]{5,4,3,2,1,0:T(8,128)(2,1)S(1)}, bf16[1,1,16,8,128,128]{5,4,3,2,1,0:T(8,128)(2,1)}, bf16[1,1,16,8,128,128]{5,4,3,2,1,0:T(8,128)(2,1)}, bf16[1,1,16,8,128,128]{5,4,3,2,1,0:T(8,128)(2,1)}) fusion(bf16[4,1,16,8,128,128]{5,4,3,2,1,0:T(8,128)(2,1)} %param.16), kind=kLoop, calls=%fused_computation.201 | loop fusion | bytes 33554432 | tf_op jit(solution)/shard_map/slice | solution.py:39
  82.5 1.9 copy-done.1
  84.7 8.7 %all-to-all-done = bf16[8,32,16,128]{3,2,0,1:T(8,128)(2,1)S(1)} async-done(((bf16[8,32,16,128]{3,2,0,1:T(8,128)(2,1)}), bf16[8,32,16,128]{3,2,0,1:T(8,128)(2,1)S(1)}, u32[]{:S(2)}, u32[]{:S(2)}) %all-to-all-start) | async-done | bytes 1048608 | tf_op jit(solution)/shard_map/all_to_all | solution.py:33
  93.3 3.0 fusion.24
  102.0 3.6 %all-to-all-start.2 = ((bf16[8,8,1,2048]{3,1,2,0:T(8,128)(2,1)}), bf16[8,8,1,2048]{3,1,2,0:T(8,128)(2,1)S(1)}, u32[]{:S(2)}, u32[]{:S(2)}) async-start(bf16[8,8,1,2048]{3,1,2,0:T(8,128)(2,1)} %constant_dynamic-update-slice_fusion), calls=%async_computation.2 | async-start | bytes 524288 | tf_op jit(solution)/shard_map/all_to_all | solution.py:69
  105.7 9.1 %all-to-all-done.2 = bf16[8,8,1,2048]{3,1,2,0:T(8,128)(2,1)S(1)} async-done(((bf16[8,8,1,2048]{3,1,2,0:T(8,128)(2,1)}), bf16[8,8,1,2048]{3,1,2,0:T(8,128)(2,1)S(1)}, u32[]{:S(2)}, u32[]{:S(2)}) %all-to-all-start.2) | async-done | bytes 262176 | tf_op jit(solution)/shard_map/all_to_all | solution.py:69
  115.0 1.8 gather_fusion.3
  117.4 0.7 select_bitcast_fusion.2
  118.1 3.6 %all-to-all-start.4 = ((bf16[8,32,1,128]{3,0,2,1:T(8,128)(2,1)}), bf16[8,32,1,128]{3,0,2,1:T(8,128)(2,1)S(1)}, u32[]{:S(2)}, u32[]{:S(2)}) async-start(bf16[8,32,1,128]{3,0,2,1:T(8,128)(2,1)} %select_bitcast_fusion.2), calls=%async_computation.4 | async-start | bytes 131072 | tf_op jit(solution)/shard_map/all_to_all | solution.py:53
  121.7 1.8 broadcast_select_fusion.2
  123.5 1.3 copy.494
  124.7 4.4 %all-to-all-done.4 = bf16[8,32,1,128]{3,0,2,1:T(8,128)(2,1)S(1)} async-done(((bf16[8,32,1,128]{3,0,2,1:T(8,128)(2,1)}), bf16[8,32,1,128]{3,0,2,1:T(8,128)(2,1)S(1)}, u32[]{:S(2)}, u32[]{:S(2)}) %all-to-all-start.4) | async-done | bytes 65568 | tf_op jit(solution)/shard_map/all_to_all | solution.py:53
  129.1 2.8 all-to-all-start.3
  134.4 0.7 gather_fusion.7
  136.4 2.5 copy_multiply_fusion.1
  138.9 2.0 copy-done.2
  141.1 16.9 %all-to-all-done.3 = bf16[8,32,16,128]{3,2,0,1:T(8,128)(2,1)S(1)} async-done(((bf16[8,32,16,128]{3,2,0,1:T(8,128)(2,1)}), bf16[8,32,16,128]{3,2,0,1:T(8,128)(2,1)S(1)}, u32[]{:S(2)}, u32[]{:S(2)}) %all-to-all-start.3) | async-done | bytes 1048608 | tf_op jit(solution)/shard_map/all_to_all | solution.py:33
  158.0 3.0 fusion.25
  166.6 3.5 %all-to-all-start.5 = ((bf16[8,8,1,2048]{3,1,2,0:T(8,128)(2,1)}), bf16[8,8,1,2048]{3,1,2,0:T(8,128)(2,1)S(1)}, u32[]{:S(2)}, u32[]{:S(2)}) async-start(bf16[8,8,1,2048]{3,1,2,0:T(8,128)(2,1)} %constant_dynamic-update-slice_fusion.8), calls=%async_computation.5 | async-start | bytes 524288 | tf_op jit(solution)/shard_map/all_to_all | solution.py:69
  170.3 9.0 %all-to-all-done.5 = bf16[8,8,1,2048]{3,1,2,0:T(8,128)(2,1)S(1)} async-done(((bf16[8,8,1,2048]{3,1,2,0:T(8,128)(2,1)}), bf16[8,8,1,2048]{3,1,2,0:T(8,128)(2,1)S(1)}, u32[]{:S(2)}, u32[]{:S(2)}) %all-to-all-start.5) | async-done | bytes 262176 | tf_op jit(solution)/shard_map/all_to_all | solution.py:69
  179.4 1.8 gather_fusion.6
  181.8 0.7 select_bitcast_fusion.1
  182.6 3.6 %all-to-all-start.7 = ((bf16[8,32,1,128]{3,0,2,1:T(8,128)(2,1)}), bf16[8,32,1,128]{3,0,2,1:T(8,128)(2,1)S(1)}, u32[]{:S(2)}, u32[]{:S(2)}) async-start(bf16[8,32,1,128]{3,0,2,1:T(8,128)(2,1)} %select_bitcast_fusion.1), calls=%async_computation.7 | async-start | bytes 131072 | tf_op jit(solution)/shard_map/all_to_all | solution.py:53
  186.2 1.8 broadcast_select_fusion.1
  188.0 1.3 copy.504
  189.3 4.3 %all-to-all-done.7 = bf16[8,32,1,128]{3,0,2,1:T(8,128)(2,1)S(1)} async-done(((bf16[8,32,1,128]{3,0,2,1:T(8,128)(2,1)}), bf16[8,32,1,128]{3,0,2,1:T(8,128)(2,1)S(1)}, u32[]{:S(2)}, u32[]{:S(2)}) %all-to-all-start.7) | async-done | bytes 65568 | tf_op jit(solution)/shard_map/all_to_all | solution.py:53
  193.6 2.6 all-to-all-start.6
  196.3 0.7 iota_reduce_fusion.5
  198.5 0.7 gather_fusion.10
  200.6 2.5 copy_multiply_fusion.2
  203.1 2.0 copy-done.3
  205.2 17.2 %all-to-all-done.6 = bf16[8,32,16,128]{3,2,0,1:T(8,128)(2,1)S(1)} async-done(((bf16[8,32,16,128]{3,2,0,1:T(8,128)(2,1)}), bf16[8,32,16,128]{3,2,0,1:T(8,128)(2,1)S(1)}, u32[]{:S(2)}, u32[]{:S(2)}) %all-to-all-start.6) | async-done | bytes 1048608 | tf_op jit(solution)/shard_map/all_to_all | solution.py:33
  222.5 3.0 fusion.26
  231.1 3.5 %all-to-all-start.8 = ((bf16[8,8,1,2048]{3,1,2,0:T(8,128)(2,1)}), bf16[8,8,1,2048]{3,1,2,0:T(8,128)(2,1)S(1)}, u32[]{:S(2)}, u32[]{:S(2)}) async-start(bf16[8,8,1,2048]{3,1,2,0:T(8,128)(2,1)} %constant_dynamic-update-slice_fusion.16), calls=%async_computation.8 | async-start | bytes 524288 | tf_op jit(solution)/shard_map/all_to_all | solution.py:69
  234.7 9.1 %all-to-all-done.8 = bf16[8,8,1,2048]{3,1,2,0:T(8,128)(2,1)S(1)} async-done(((bf16[8,8,1,2048]{3,1,2,0:T(8,128)(2,1)}), bf16[8,8,1,2048]{3,1,2,0:T(8,128)(2,1)S(1)}, u32[]{:S(2)}, u32[]{:S(2)}) %all-to-all-start.8) | async-done | bytes 262176 | tf_op jit(solution)/shard_map/all_to_all | solution.py:69
  244.0 1.8 gather_fusion.9
  246.4 0.7 select_bitcast_fusion
  247.1 3.6 %all-to-all-start.10 = ((bf16[8,32,1,128]{3,0,2,1:T(8,128)(2,1)}), bf16[8,32,1,128]{3,0,2,1:T(8,128)(2,1)S(1)}, u32[]{:S(2)}, u32[]{:S(2)}) async-start(bf16[8,32,1,128]{3,0,2,1:T(8,128)(2,1)} %select_bitcast_fusion), calls=%async_computation.10 | async-start | bytes 131072 | tf_op jit(solution)/shard_map/all_to_all | solution.py:53
  250.7 1.8 broadcast_select_fusion
  252.5 1.2 copy.514
  253.7 4.4 %all-to-all-done.10 = bf16[8,32,1,128]{3,0,2,1:T(8,128)(2,1)S(1)} async-done(((bf16[8,32,1,128]{3,0,2,1:T(8,128)(2,1)}), bf16[8,32,1,128]{3,0,2,1:T(8,128)(2,1)S(1)}, u32[]{:S(2)}, u32[]{:S(2)}) %all-to-all-start.10) | async-done | bytes 65568 | tf_op jit(solution)/shard_map/all_to_all | solution.py:53
  258.1 2.9 all-to-all-start.9
  261.0 0.7 iota_reduce_fusion.4
  264.2 2.5 copy_multiply_fusion.3
  266.8 1.9 copy-done
  268.9 18.1 %all-to-all-done.9 = bf16[8,32,16,128]{3,2,0,1:T(8,128)(2,1)S(1)} async-done(((bf16[8,32,16,128]{3,2,0,1:T(8,128)(2,1)}), bf16[8,32,16,128]{3,2,0,1:T(8,128)(2,1)S(1)}, u32[]{:S(2)}, u32[]{:S(2)}) %all-to-all-start.9) | async-done | bytes 1048608 | tf_op jit(solution)/shard_map/all_to_all | solution.py:33
  287.0 3.0 fusion.27
  290.7 12.5 %all_to_all.60 = bf16[8,8,1,2048]{3,1,2,0:T(8,128)(2,1)S(1)} all-to-all(bf16[8,8,1,2048]{3,1,2,0:T(8,128)(2,1)S(1)} %constant_dynamic-update-slice_fusion.24), channel_id=1, replica_groups=mesh['gx'=8,'gy'=4] {'gx'}, dimensions={0} | all-to-all | bytes 524288 | tf_op jit(solution)/shard_map/all_to_all | solution.py:69
  303.2 0.7 copy.683
  (134 shorter events, 29.2 us)
Async XLA Ops:
  51.4 10.0 %all-to-all-start.1 = ((bf16[8,32,1,128]{3,0,2,1:T(8,128)(2,1)}), bf16[8,32,1,128]{3,0,2,1:T(8,128)(2,1)S(1)}, u32[]{:S(2)}, u32[]{:S(2)}) async-start(bf16[8,32,1,128]{3,0,2,1:T(8,128)(2,1)} %select_bitcast_fusion.3), calls=%async_computation.1 | async-start | bytes 131072 | tf_op jit(solution)/shard_map/all_to_all | solution.py:53
  56.2 14.9 %copy-start.4 = (f32[4,1,16,128]{3,2,1,0:T(8,128)S(1)}, f32[4,1,16,128]{3,2,1,0:T(8,128)}, u32[]{:S(2)}) copy-start(f32[4,1,16,128]{3,2,1,0:T(8,128)} %param.17) | copy-start | bytes 98308
  61.4 31.9 %all-to-all-start = ((bf16[8,32,16,128]{3,2,0,1:T(8,128)(2,1)}), bf16[8,32,16,128]{3,2,0,1:T(8,128)(2,1)S(1)}, u32[]{:S(2)}, u32[]{:S(2)}) async-start(bf16[8,32,16,128]{3,2,0,1:T(8,128)(2,1)} %copy.483), calls=%async_computation | async-start | bytes 2097152 | tf_op jit(solution)/shard_map/all_to_all | solution.py:33
  82.5 2.0 copy-start.1
  102.0 12.8 %all-to-all-start.2 = ((bf16[8,8,1,2048]{3,1,2,0:T(8,128)(2,1)}), bf16[8,8,1,2048]{3,1,2,0:T(8,128)(2,1)S(1)}, u32[]{:S(2)}, u32[]{:S(2)}) async-start(bf16[8,8,1,2048]{3,1,2,0:T(8,128)(2,1)} %constant_dynamic-update-slice_fusion), calls=%async_computation.2 | async-start | bytes 524288 | tf_op jit(solution)/shard_map/all_to_all | solution.py:69
  115.0 17.0 %copy-start.5 = (s32[4,1,16]{2,1,0:T(1,128)S(1)}, s32[4,1,16]{2,1,0:T(1,128)}, u32[]{:S(2)}) copy-start(s32[4,1,16]{2,1,0:T(1,128)} %param.15) | copy-start | bytes 772
  118.1 11.0 %all-to-all-start.4 = ((bf16[8,32,1,128]{3,0,2,1:T(8,128)(2,1)}), bf16[8,32,1,128]{3,0,2,1:T(8,128)(2,1)S(1)}, u32[]{:S(2)}, u32[]{:S(2)}) async-start(bf16[8,32,1,128]{3,0,2,1:T(8,128)(2,1)} %select_bitcast_fusion.2), calls=%async_computation.4 | async-start | bytes 131072 | tf_op jit(solution)/shard_map/all_to_all | solution.py:53
  129.1 28.8 %all-to-all-start.3 = ((bf16[8,32,16,128]{3,2,0,1:T(8,128)(2,1)}), bf16[8,32,16,128]{3,2,0,1:T(8,128)(2,1)S(1)}, u32[]{:S(2)}, u32[]{:S(2)}) async-start(bf16[8,32,16,128]{3,2,0,1:T(8,128)(2,1)} %copy.494), calls=%async_computation.3 | async-start | bytes 2097152 | tf_op jit(solution)/shard_map/all_to_all | solution.py:33
  138.9 2.0 copy-start.2
  166.6 12.7 %all-to-all-start.5 = ((bf16[8,8,1,2048]{3,1,2,0:T(8,128)(2,1)}), bf16[8,8,1,2048]{3,1,2,0:T(8,128)(2,1)S(1)}, u32[]{:S(2)}, u32[]{:S(2)}) async-start(bf16[8,8,1,2048]{3,1,2,0:T(8,128)(2,1)} %constant_dynamic-update-slice_fusion.8), calls=%async_computation.5 | async-start | bytes 524288 | tf_op jit(solution)/shard_map/all_to_all | solution.py:69
  182.6 11.0 %all-to-all-start.7 = ((bf16[8,32,1,128]{3,0,2,1:T(8,128)(2,1)}), bf16[8,32,1,128]{3,0,2,1:T(8,128)(2,1)S(1)}, u32[]{:S(2)}, u32[]{:S(2)}) async-start(bf16[8,32,1,128]{3,0,2,1:T(8,128)(2,1)} %select_bitcast_fusion.1), calls=%async_computation.7 | async-start | bytes 131072 | tf_op jit(solution)/shard_map/all_to_all | solution.py:53
  193.6 28.8 %all-to-all-start.6 = ((bf16[8,32,16,128]{3,2,0,1:T(8,128)(2,1)}), bf16[8,32,16,128]{3,2,0,1:T(8,128)(2,1)S(1)}, u32[]{:S(2)}, u32[]{:S(2)}) async-start(bf16[8,32,16,128]{3,2,0,1:T(8,128)(2,1)} %copy.504), calls=%async_computation.6 | async-start | bytes 2097152 | tf_op jit(solution)/shard_map/all_to_all | solution.py:33
  203.1 2.0 copy-start.3
  231.1 12.7 %all-to-all-start.8 = ((bf16[8,8,1,2048]{3,1,2,0:T(8,128)(2,1)}), bf16[8,8,1,2048]{3,1,2,0:T(8,128)(2,1)S(1)}, u32[]{:S(2)}, u32[]{:S(2)}) async-start(bf16[8,8,1,2048]{3,1,2,0:T(8,128)(2,1)} %constant_dynamic-update-slice_fusion.16), calls=%async_computation.8 | async-start | bytes 524288 | tf_op jit(solution)/shard_map/all_to_all | solution.py:69
  247.1 11.0 %all-to-all-start.10 = ((bf16[8,32,1,128]{3,0,2,1:T(8,128)(2,1)}), bf16[8,32,1,128]{3,0,2,1:T(8,128)(2,1)S(1)}, u32[]{:S(2)}, u32[]{:S(2)}) async-start(bf16[8,32,1,128]{3,0,2,1:T(8,128)(2,1)} %select_bitcast_fusion), calls=%async_computation.10 | async-start | bytes 131072 | tf_op jit(solution)/shard_map/all_to_all | solution.py:53
  258.1 28.8 %all-to-all-start.9 = ((bf16[8,32,16,128]{3,2,0,1:T(8,128)(2,1)}), bf16[8,32,16,128]{3,2,0,1:T(8,128)(2,1)S(1)}, u32[]{:S(2)}, u32[]{:S(2)}) async-start(bf16[8,32,16,128]{3,2,0,1:T(8,128)(2,1)} %copy.514), calls=%async_computation.9 | async-start | bytes 2097152 | tf_op jit(solution)/shard_map/all_to_all | solution.py:33
  266.8 1.9 copy-start
